TPU v7x, 32 devices: a whole 2x2x4 slice. The times are simulated.
32 devices in a mesh: dp: 4 (over y, core), seq: 8 (over z, x).
Axes of the slice: x: 2, y: 2, z: 4, core: 2. Of those that a mesh axis runs over, the one named last changes fastest.
Arguments:
- mixer_in: bfloat16 [4, 2048, 2560], P('dp', 'seq'), may hold values from -6 to 6
- step_raw: float32 [4, 40, 2048], P('dp', None, 'seq'), may hold values from -3 to 3
- key_proj: bfloat16 [4, 2048, 128], P('dp', 'seq'), may hold values from -0.3125 to 0.3125
- query_proj: bfloat16 [4, 2048, 128], P('dp', 'seq'), may hold values from -0.3125 to 0.3125
- codec_ids: int32 [4, 2048], P('dp', 'seq'), may hold values from 0 to 1023
- finger_ids: int32 [4, 2048], P('dp', 'seq'), may hold values from 0 to 4, as said below
- fret_ids: int32 [4, 2048], P('dp', 'seq'), may hold values from 0 to 24, as said below
- grad_out: bfloat16 [4, 2048, 2560], P('dp', 'seq'), may hold values from -12 to 12
- decay_log: float32 [40], replicated, may hold values from -16 to 1
- skip_gain: float32 [40], replicated, may hold values from 0.5 to 1.5
- codec_bias: float32 [40, 1024], replicated, may hold values from -1.75 to 1.75
- fret_bias: float32 [40, 25], replicated, may hold values from -1.75 to 1.75
- finger_damp: float32 [40, 5], replicated, may hold values from -1.4 to -0.4
Outputs:
- grad_mixer_in: bfloat16 [4, 2048, 2560], P('dp', 'seq')
- grad_step_raw: float32 [4, 40, 2048], P('dp', None, 'seq')
- grad_key_proj: bfloat16 [4, 2048, 128], P('dp', 'seq')
- grad_query_proj: bfloat16 [4, 2048, 128], P('dp', 'seq')
- grad_decay_log: float32 [40], replicated
- grad_skip_gain: float32 [40], replicated
- grad_codec_bias: float32 [40, 1024], replicated
- grad_fret_bias: float32 [40, 25], replicated
- grad_finger_damp: float32 [40, 5], replicated
Inputs may be any that keep to these rules, and one draw needn't show every extreme that they name: `finger_ids`: each sequence's finger and fret ids are constant over 4 runs of positions that follow one another; the 3 positions where a run begins are drawn afresh for every sequence, one of them at a multiple of 256 where the finger changes; other neighbouring runs may share ids. `fret_ids`: constant over the same runs as finger_ids.
All inputs are finite; a program needn't handle non-finite values.
Results may differ from a plain program's by a relative error of at most 0.0057.
Values sent between devices are 32-bit elements; how exact they have to be, the bound alone decides.
A program may use at most 192 MiB of HBM per device.

v0:
```python
import jax
import jax.numpy as jnp
from jax import lax
from jax.sharding import PartitionSpec as P

STRETCH = 256


block_heads = 8


def shifted(value, axis, by):
    count = lax.axis_size(axis)
    pairs = [(i, i + by) for i in range(count) if 0 <= i + by < count]
    return lax.ppermute(value, axis, pairs)


def entering_2(value, axis, join, neutral, backward):
    count, mine = (lax.axis_size(axis), lax.axis_index(axis))
    pieces = jax.tree.map(lambda part: lax.all_gather(part, axis), value)
    if backward:
        pieces = jax.tree.map(lambda part: part[::-1], pieces)
        mine = count - 1 - mine
    running = jax.tree.map(
        lambda part, zero: jnp.full_like(part, 0) + jnp.asarray(zero, part.dtype), value, neutral
    )

    def lap(position, running):
        longer = join(running, jax.tree.map(lambda part: part[position], pieces))
        return jax.tree.map(lambda new, old: jnp.where(position < mine, new, old), longer, running)

    return lax.fori_loop(0, count - 1, lap, running)


def product(form, left, right):
    return jnp.einsum(form, left, right, preferred_element_type=jnp.float32)


def combine(earlier, later):
    return (earlier[0] + later[0], jnp.exp(later[0])[:, None, None] * earlier[1] + later[1])


def advance(carry, parts):
    return (jnp.exp(parts[0])[:, None, None] * carry + parts[1], carry)


def fold_step(carry, parts):
    return (combine(carry, parts), None)


def stretch_state(mixer_stretch, key_stretch, step_stretch, cum_stretch):
    length = mixer_stretch.shape[0]
    head_count = step_stretch.shape[0]
    tail_weight = jnp.exp(cum_stretch[:, -1:] - cum_stretch) * step_stretch
    weighted = (mixer_stretch.reshape(length, head_count, -1) * tail_weight.T[:, :, None]).astype(
        jnp.bfloat16
    )
    return product("lhp,ln->hpn", weighted, key_stretch)


def stretch_pull(grad_stretch, query_stretch, cum_stretch):
    length = grad_stretch.shape[0]
    head_count = cum_stretch.shape[0]
    weighted = (
        grad_stretch.reshape(length, head_count, -1) * jnp.exp(cum_stretch).T[:, :, None]
    ).astype(jnp.bfloat16)
    return product("lhp,ln->hpn", weighted, query_stretch)


def stretch_grads(
    mixer_stretch,
    key_stretch,
    query_stretch,
    grad_stretch,
    step_stretch,
    cum_stretch,
    state_in,
    state_grad,
    skip_gain,
):
    length, feature_width = mixer_stretch.shape
    head_count = step_stretch.shape[0]
    groups = head_count // block_heads
    head_dim = feature_width // head_count
    state_dim = key_stretch.shape[1]
    row_index = jnp.arange(length)
    causal = row_index[:, None] >= row_index[None, :]
    gram_block = jnp.dot(query_stretch, key_stretch.T, preferred_element_type=jnp.float32)
    query_wide = query_stretch.astype(jnp.float32)

    def one_group(carry, parts):
        gram_grad, query_extra, key_extra = carry
        mixer_group, grad_group, step_group, cum_group, state_group, pull_group, skip_group = parts
        gap_log = cum_group[:, :, None] - cum_group[:, None, :]
        decay_part = jnp.exp(jnp.where(causal[None], gap_log, -jnp.inf))
        step_cols = step_group[:, None, :]
        weights = (gram_block[None] * decay_part * step_cols).astype(jnp.bfloat16)
        diag_grad = product("hij,ihp->jhp", weights, grad_group)
        grad_weights = product("ihp,jhp->hij", grad_group, mixer_group)
        masked = grad_weights * decay_part
        gram_grad = gram_grad + jnp.sum(masked * step_cols, axis=0)
        grad_step = jnp.sum(masked * gram_block[None], axis=1)
        row_cross = jnp.sum(masked * gram_block[None] * step_cols, axis=2)
        grad_cum = row_cross - step_group * grad_step
        state_low = state_group.astype(jnp.bfloat16)
        state_read = product("ihp,hpn->hin", grad_group, state_low)
        rise_factor = jnp.exp(cum_group)
        query_extra = query_extra + jnp.sum(rise_factor[:, :, None] * state_read, axis=0)
        grad_cum = grad_cum + rise_factor * jnp.sum(state_read * query_wide[None], axis=2)
        block_total = cum_group[:, -1]
        tail_decay = jnp.exp(block_total[:, None] - cum_group)
        tail_weight = tail_decay * step_group
        grad_low = pull_group.astype(jnp.bfloat16)
        pulled_rows = product("ln,hpn->lhp", key_stretch, grad_low)
        grad_tail = jnp.sum(mixer_group.astype(jnp.float32) * pulled_rows, axis=2).T
        mixed_state = product("lhp,hpn->hln", mixer_group, grad_low)
        key_extra = key_extra + jnp.sum(tail_weight[:, :, None] * mixed_state, axis=0)
        tail_grad = grad_tail * tail_weight
        total_grad = jnp.sum(tail_grad, axis=1) + jnp.exp(block_total) * jnp.sum(
            pull_group * state_group, axis=(1, 2)
        )
        grad_cum = grad_cum - tail_grad
        grad_cum = grad_cum.at[:, -1].add(total_grad)
        grad_step = grad_step + grad_tail * tail_decay
        grad_mixer = (
            diag_grad
            + tail_weight.T[:, :, None] * pulled_rows
            + skip_group[None, :, None] * grad_group.astype(jnp.float32)
        )
        return ((gram_grad, query_extra, key_extra), (grad_mixer, grad_step, grad_cum))

    parts = (
        mixer_stretch.reshape(length, groups, block_heads, head_dim).transpose(1, 0, 2, 3),
        grad_stretch.reshape(length, groups, block_heads, head_dim).transpose(1, 0, 2, 3),
        step_stretch.reshape(groups, block_heads, length),
        cum_stretch.reshape(groups, block_heads, length),
        state_in.reshape(groups, block_heads, head_dim, state_dim),
        state_grad.reshape(groups, block_heads, head_dim, state_dim),
        skip_gain.reshape(groups, block_heads),
    )
    start = (
        jnp.zeros((length, length), jnp.float32),
        jnp.zeros((length, state_dim), jnp.float32),
        jnp.zeros((length, state_dim), jnp.float32),
    )
    (gram_grad, query_extra, key_extra), (mixer_grads, step_grads, cum_grads) = lax.scan(
        one_group, start, parts
    )
    gram_low = gram_grad.astype(jnp.bfloat16)
    grad_query = jnp.dot(gram_low, key_stretch, preferred_element_type=jnp.float32) + query_extra
    grad_key = jnp.dot(gram_low.T, query_stretch, preferred_element_type=jnp.float32) + key_extra
    grad_mixer = mixer_grads.transpose(1, 0, 2, 3).reshape(length, feature_width)
    return (
        grad_mixer,
        grad_key,
        grad_query,
        step_grads.reshape(head_count, length),
        cum_grads.reshape(head_count, length),
    )


def shards(
    mixer_in,
    step_raw,
    key_proj,
    query_proj,
    codec_ids,
    finger_ids,
    fret_ids,
    grad_out,
    decay_log,
    skip_gain,
    codec_bias,
    fret_bias,
    finger_damp,
):
    tokens = mixer_in.shape[1]
    feature_width = mixer_in.shape[2]
    head_count = decay_log.shape[0]
    head_dim = feature_width // head_count
    state_dim = key_proj.shape[2]
    stretches = tokens // STRETCH
    highest = lax.Precision.HIGHEST
    fingers = finger_ids[0]
    frets = fret_ids[0]
    codec_row = codec_ids[0]
    latest = jnp.stack([fingers[-1], frets[-1]])
    before = shifted(latest, "seq", 1)
    prior_finger = jnp.concatenate([before[0:1], fingers[:-1]])
    prior_fret = jnp.concatenate([before[1:2], frets[:-1]])
    position = lax.axis_index("seq") * tokens + jnp.arange(tokens, dtype=jnp.int32)
    changed = ((fingers != prior_finger) | (frets != prior_fret)).astype(jnp.float32)
    onset_mask = jnp.where(position == 0, 0.0, changed)
    codec_hot = (
        jnp.arange(codec_bias.shape[1], dtype=jnp.int32)[:, None] == codec_row[None, :]
    ).astype(jnp.float32)
    fret_hot = (jnp.arange(fret_bias.shape[1], dtype=jnp.int32)[:, None] == frets[None, :]).astype(
        jnp.float32
    )
    finger_hot = (
        jnp.arange(finger_damp.shape[1], dtype=jnp.int32)[:, None] == fingers[None, :]
    ).astype(jnp.float32)
    pre_step = (
        step_raw[0]
        + jnp.dot(codec_bias, codec_hot, precision=highest)
        + jnp.dot(fret_bias, fret_hot, precision=highest)
    )
    step_size = jax.nn.softplus(pre_step)
    damping = jnp.dot(jax.nn.softplus(finger_damp), finger_hot, precision=highest)
    decay_rate = jnp.exp(decay_log)
    log_decay = -decay_rate[:, None] * step_size - onset_mask[None, :] * damping
    step_blocks = step_size.reshape(head_count, stretches, STRETCH).transpose(1, 0, 2)
    cum_blocks = jnp.cumsum(
        log_decay.reshape(head_count, stretches, STRETCH).transpose(1, 0, 2), axis=2
    )
    mixer_blocks = mixer_in[0].reshape(stretches, STRETCH, feature_width)
    grad_blocks = grad_out[0].reshape(stretches, STRETCH, feature_width)
    key_blocks = key_proj[0].reshape(stretches, STRETCH, state_dim)
    query_blocks = query_proj[0].reshape(stretches, STRETCH, state_dim)
    totals = cum_blocks[:, :, -1]
    states = lax.map(
        lambda items: stretch_state(*items), (mixer_blocks, key_blocks, step_blocks, cum_blocks)
    )
    block_pulls = lax.map(
        lambda items: stretch_pull(*items), (grad_blocks, query_blocks, cum_blocks)
    )
    empty_state = jnp.zeros((head_count, head_dim, state_dim), jnp.float32)
    empty_total = jnp.zeros((head_count,), jnp.float32)
    own_forward = lax.scan(fold_step, (empty_total, empty_state), (totals, states))[0]
    own_backward = lax.scan(
        fold_step, (empty_total, empty_state), (totals, block_pulls), reverse=True
    )[0]
    entering = entering_2(own_forward, "seq", combine, (empty_total, empty_state), False)[1]
    leaving = entering_2(own_backward, "seq", combine, (empty_total, empty_state), True)[1]
    state_ins = lax.scan(advance, entering, (totals, states))[1]
    state_grads = lax.scan(advance, leaving, (totals, block_pulls), reverse=True)[1]
    outcome = lax.map(
        lambda items: stretch_grads(*items, skip_gain),
        (
            mixer_blocks,
            key_blocks,
            query_blocks,
            grad_blocks,
            step_blocks,
            cum_blocks,
            state_ins,
            state_grads,
        ),
    )
    grad_mixer, grad_key, grad_query, grad_step, grad_cum = outcome
    grad_log = jnp.flip(jnp.cumsum(jnp.flip(grad_cum, 2), 2), 2)
    grad_log = grad_log.transpose(1, 0, 2).reshape(head_count, tokens)
    grad_step = grad_step.transpose(1, 0, 2).reshape(head_count, tokens)
    grad_pre = (grad_step - decay_rate[:, None] * grad_log) * jax.nn.sigmoid(pre_step)
    grad_decay = -decay_rate * jnp.sum(step_size * grad_log, axis=1)
    grad_damp = jnp.dot(
        -(onset_mask[None, :] * grad_log), finger_hot.T, precision=highest
    ) * jax.nn.sigmoid(finger_damp)
    grad_codec = jnp.dot(grad_pre, codec_hot.T, precision=highest)
    grad_fret = jnp.dot(grad_pre, fret_hot.T, precision=highest)
    grad_skip = product(
        "lhp,lhp->h",
        mixer_in[0].reshape(tokens, head_count, head_dim),
        grad_out[0].reshape(tokens, head_count, head_dim),
    )
    small_grads = (grad_skip, grad_decay, grad_damp, grad_codec, grad_fret)
    small_grads = lax.psum(
        (small_grads[0], small_grads[1], small_grads[2], small_grads[3], small_grads[4]),
        ("dp", "seq"),
    )
    grad_scale = (lax.axis_size("dp") * lax.axis_size("seq") * tokens) ** (-0.5)
    return (
        grad_mixer.astype(jnp.bfloat16),
        grad_pre[None],
        grad_key.astype(jnp.bfloat16),
        grad_query.astype(jnp.bfloat16),
        small_grads[1] * grad_scale,
        small_grads[0] * grad_scale,
        small_grads[3] * grad_scale,
        small_grads[4] * grad_scale,
        small_grads[2] * grad_scale,
    )


def solution(mesh):
    in_specs = (
        P("dp", "seq", None),
        P("dp", None, "seq"),
        P("dp", "seq", None),
        P("dp", "seq", None),
        P("dp", "seq"),
        P("dp", "seq"),
        P("dp", "seq"),
        P("dp", "seq", None),
        P(),
        P(),
        P(),
        P(),
        P(),
    )
    out_specs = (
        P("dp", "seq", None),
        P("dp", None, "seq"),
        P("dp", "seq", None),
        P("dp", "seq", None),
        P(),
        P(),
        P(),
        P(),
        P(),
    )
    return jax.shard_map(shards, mesh=mesh, in_specs=in_specs, out_specs=out_specs, check_vma=False)
```

profile of v0, /device:TPU:0, one launch (start us, length us, event | category | flops | bytes accessed | tf_op | source)
XLA Modules:
  0.0 603.9 jit_solution(9062517489203797136)
XLA Ops:
  11.1 4.9 collective-permute-start
  17.2 1.7 copy.128
  25.4 1.7 convolution_add_fusion.1
  30.1 1.6 convolution_add_fusion
  35.2 3.1 fusion.44
  38.4 19.9 %all-gather = f32[8,40,1]{1,2,0:T(1,128)S(1)} all-gather(f32[1,40,1]{1,2,0:T(1,128)S(1)} %copy.133), channel_id=2, replica_groups=mesh['dp'=4,'seq'=8] {'seq'}, dimensions={0}, use_global_device_ids=true | all-gather | bytes 1440 | tf_op jit(solution)/shard_map/all_gather | solution.py:20
  59.0 119.1 %all-gather.6.cloned.1.call-done = f32[320,64,128]{2,1,0:T(8,128)} async-done(((f32[40,64,128]{2,1,0:T(8,128)}), f32[320,64,128]{2,1,0:T(8,128)}) %all-gather.6.cloned.1.call-update) | async-done | bytes 10485776 | tf_op jit(solution)/shard_map/all_gather | solution.py:20
  178.0 12.1 %while.42 = (s32[]{:T(128)}, f32[40,64,128]{2,1,0:T(8,128)S(1)}, s32[]{:T(128)}, f32[8,40]{1,0:T(8,128)S(1)}, f32[8,40,64,128]{3,2,1,0:T(8,128)}, /*index=5*/s32[]{:T(128)}, s32[]{:T(128)}) while((s32[]{:T(128)}, f32[40,64,128]{2,1,0:T(8,128)S(1)}, s32[]{:T(128)}, f32[8,40]{1,0:T(8,128)S(1)}, f32[8,40,64,128]{3,2,1,0:T(8,128)}, ...), condition=%wide.region_3.4_spmd.clone, body=%wide.region_2.3_spmd.clone.sunk | while | flops 1310724 | bytes 3932745 | solution.py:32
  178.1 1.6 fusion.108
  179.7 1.6 fusion.108
  181.4 1.6 fusion.108
  183.0 1.6 fusion.108
  184.7 1.8 fusion.108
  186.5 1.8 fusion.108
  188.3 1.8 fusion.108
  190.2 138.8 %all-gather.8.cloned.1.call-done = f32[320,64,128]{2,1,0:T(8,128)} async-done(((f32[40,64,128]{2,1,0:T(8,128)}), f32[320,64,128]{2,1,0:T(8,128)}) %all-gather.8.cloned.1.call-update) | async-done | bytes 10485776 | tf_op jit(solution)/shard_map/all_gather | solution.py:20
  329.0 10.2 %rev.14 = f32[8,40,64,128]{3,2,1,0:T(8,128)} reverse(f32[8,40,64,128]{3,2,1,0:T(8,128)} %bitcast.277), dimensions={0} | reverse | bytes 20971520 | tf_op jit(solution)/shard_map/rev | solution.py:22
  339.1 11.6 %while.43 = (s32[]{:T(128)}, f32[40,64,128]{2,1,0:T(8,128)S(1)}, s32[]{:T(128)}, f32[8,40]{1,0:T(8,128)S(1)}, f32[8,40,64,128]{3,2,1,0:T(8,128)}, /*index=5*/s32[]{:T(128)}, s32[]{:T(128)}) while((s32[]{:T(128)}, f32[40,64,128]{2,1,0:T(8,128)S(1)}, s32[]{:T(128)}, f32[8,40]{1,0:T(8,128)S(1)}, f32[8,40,64,128]{3,2,1,0:T(8,128)}, ...), condition=%wide.region_5.6_spmd.clone, body=%wide.region_4.5_spmd.clone.sunk | while | flops 1310724 | bytes 3932745 | solution.py:32
  339.1 1.6 fusion.109
  340.8 1.6 fusion.109
  342.5 1.6 fusion.109
  344.1 1.6 fusion.109
  345.8 1.6 fusion.109
  347.4 1.6 fusion.109
  349.1 1.6 fusion.109
  350.7 116.2 %while.44 = (s32[]{:T(128)}, f32[256,256]{1,0:T(8,128)}, f32[256,128]{0,1:T(8,128)S(1)}, f32[256,128]{1,0:T(8,128)}, bf16[5,256,8,64]{1,3,2,0:T(8,128)(2,1)}, /*...) while((s32[]{:T(128)}, f32[256,256]{1,0:T(8,128)}, ...), condition=%wide.region_17.18_spmd.clone, body=%wide.region_7.17_spmd.clone.sunk | while | flops 245188640 | bytes 9993798 | solution.py:146
  352.8 1.4 fusion.114
  354.3 3.1 multiply_reduce_fusion.13
  357.4 2.0 multiply_reduce_fusion.14
  362.7 2.0 fusion.118
  367.4 2.6 fusion.117
  370.0 1.7 select_add_fusion.6
  371.7 1.5 fusion.115
  377.5 3.1 multiply_reduce_fusion.13
  380.6 2.0 multiply_reduce_fusion.14
  385.9 2.0 fusion.118
  390.6 2.6 fusion.117
  393.2 1.8 select_add_fusion.6
  395.0 1.5 fusion.115
  400.7 3.1 multiply_reduce_fusion.13
  403.9 2.0 multiply_reduce_fusion.14
  409.2 2.0 fusion.118
  413.9 2.6 fusion.117
  416.4 1.8 select_add_fusion.6
  418.3 1.5 fusion.115
  422.5 1.4 fusion.114
  424.0 3.1 multiply_reduce_fusion.13
  427.1 2.0 multiply_reduce_fusion.14
  432.4 2.0 fusion.118
  437.1 2.6 fusion.117
  439.7 1.8 select_add_fusion.6
  441.5 1.5 fusion.115
  445.8 1.4 fusion.114
  447.2 3.1 multiply_reduce_fusion.13
  450.4 2.0 multiply_reduce_fusion.14
  455.7 2.0 fusion.118
  460.4 2.6 fusion.117
  463.0 1.8 select_add_fusion.6
  464.8 1.5 fusion.115
  470.2 2.0 fusion.54
  473.9 38.7 %all-reduce = (f32[40]{0:T(128)S(1)}, f32[40]{0:T(128)S(1)}, f32[40,25]{0,1:T(8,128)S(1)}, f32[40,5]{0,1:T(8,128)S(1)}) all-reduce(f32[40]{0:T(128)S(1)} %negate_multiply_fusion, f32[40]{0:T(128)S(1)} %copy-done.23, f32[40,25]{0,1:T(8,128)S(1)} %fusion.69, ...), channel_id=1, replica_groups=mesh['dp'=4,'seq'=8] {'dp','seq'}, use_global_device_ids=true, to_apply=%region_21.22 | all-reduce | flops 1280 | bytes 10240 | tf_op jit(solution)/shard_map/psum | solution.py:267
  514.0 1.6 copy.145
  517.8 77.9 %all-reduce.3.cloned.1.call-done = f32[40,1024]{1,0:T(8,128)} async-done(((f32[40,1024]{1,0:T(8,128)}), f32[40,1024]{1,0:T(8,128)}) %all-reduce.3.cloned.1.call-update) | async-done | bytes 163856 | tf_op jit(solution)/shard_map/psum | solution.py:267
  595.7 1.6 broadcast_multiply_fusion
  (258 shorter events, 74.0 us)
Async XLA Ops:
  7.2 11.7 %copy-start = (f32[40,1024]{1,0:T(8,128)S(1)}, f32[40,1024]{1,0:T(8,128)}, u32[]{:S(2)}) copy-start(f32[40,1024]{1,0:T(8,128)} %param.31) | copy-start | bytes 491524
  7.2 170.9 %all-gather.6.cloned.1.call-start = ((), (), s32[]{:S(2)}) async-start(), calls=%async_computation.1 | async-start | bytes 11796480 | tf_op jit(solution)/shard_map/all_gather | solution.py:20
  11.1 8.5 %collective-permute-start = (s32[2]{0:T(128)S(1)}, s32[2]{0:T(128)S(1)}, u32[]{:S(2)}, u32[]{:S(2)}) collective-permute-start(s32[2]{0:T(128)S(1)} %pad_add_fusion), channel_id=1, source_target_pairs={{0,1},{1,2},{2,3},{3,4},{4,5},{5,6},{6,7},{8,9},{9,10},{10,11},{11... | collective-permute-start | bytes 32 | tf_op jit(solution)/shard_map/ppermute | solution.py:15
  17.1 1.7 copy-start.25
  17.2 1.7 copy-start.26
  17.2 2.2 copy-start.18
  17.2 2.2 copy-start.19
  17.2 3.0 copy-start.20
  17.2 5.0 copy-start.21
  18.8 5.8 copy-start.1
  19.6 5.1 copy-start.14
  21.6 0.6 copy-start.22
  24.4 1.0 copy-start.7
  27.0 1.3 copy-start.10
  27.1 301.9 %all-gather.8.cloned.1.call-start = ((), (), s32[]{:S(2)}) async-start(), calls=%async_computation.2 | async-start | bytes 11796480 | tf_op jit(solution)/shard_map/all_gather | solution.py:20
  29.0 1.1 copy-start.3
  29.0 1.1 copy-start.12
  31.6 0.7 copy-start.24
  31.7 564.1 %all-reduce.3.cloned.1.call-start = ((), (), s32[]{:S(2)}) async-start(), calls=%async_computation | async-start | bytes 327680 | tf_op jit(solution)/shard_map/psum | solution.py:267
  352.8 1.4 copy-start.17
  354.3 3.2 copy-start.9
  354.3 3.2 copy-start.16
  370.0 3.2 copy-start.4
  370.0 3.3 copy-start.8
  373.3 0.6 copy-start.5
  376.0 1.4 copy-start.17
  377.4 3.2 copy-start.9
  377.4 3.2 copy-start.16
  393.2 3.3 copy-start.4
  393.2 3.4 copy-start.8
  396.5 0.6 copy-start.5
  399.2 1.4 copy-start.17
  400.7 3.2 copy-start.9
  400.7 3.2 copy-start.16
  416.4 3.3 copy-start.4
  416.4 3.4 copy-start.8
  419.8 0.6 copy-start.5
  422.5 1.4 copy-start.17
  424.0 3.2 copy-start.9
  424.0 3.2 copy-start.16
  439.7 3.3 copy-start.4
  439.7 3.4 copy-start.8
  443.0 0.6 copy-start.5
  445.8 1.4 copy-start.17
  447.2 3.2 copy-start.9
  447.2 3.2 copy-start.16
  463.0 3.3 copy-start.4
  463.0 3.4 copy-start.8
  466.3 0.6 copy-start.5
  466.9 7.0 %copy-start.27 = (f32[40]{0:T(128)S(1)}, f32[40]{0:T(128)}, u32[]{:S(2)}) copy-start(f32[40]{0:T(128)} %param.29) | copy-start | bytes 484
  467.0 7.0 %copy-start.23 = (f32[40]{0:T(128)S(1)}, f32[40]{0:T(128)}, u32[]{:S(2)}) copy-start(f32[40]{0:T(128)} %fusion.44) | copy-start | bytes 484
  467.0 47.0 %copy-start.11 = (bf16[5,256,8,64]{1,3,2,0:T(8,128)(2,1)S(1)}, bf16[5,256,8,64]{1,3,2,0:T(8,128)(2,1)}, u32[]{:S(2)}) copy-start(bf16[5,256,8,64]{1,3,2,0:T(8,128)(2,1)} %get-tuple-element.638) | copy-start | bytes 3932164
  470.2 45.4 %copy-start.15 = (f32[40,256]{1,0:T(8,128)}, f32[40,256]{1,0:T(8,128)S(1)}, u32[]{:S(2)}) copy-start(f32[40,256]{1,0:T(8,128)S(1)} %get-tuple-element.918) | copy-start | bytes 122884
  514.0 2.1 copy-start.2
  514.0 2.9 copy-start.6
  514.0 2.9 copy-start.13
Sparse Core Ops, SparseCore 0:
  27.2 150.8 all-gather.5
  180.2 148.6 all-gather.7
  474.0 121.6 all-reduce.2
where the time goes:
time: 608 us; the launch traced here: 604 us
  waiting for transfers between devices  336 us (55%)
  other arithmetic  75.7 us (12%)
  matrix products  62.1 us (10%)
  blocking collectives  58.6 us (10%)
  local copies, waits for them, and re-layouts  51.5 us (8%)
  between operations  14.2 us (2%)
    all_gather x2, waiting for transfers between devices, entering_2(): pieces = jax.tree.map(lambda part: lax.all_gather(part, axis), value)  258 us
    psum x1, waiting for transfers between devices, shards(): lax.psum((small_grads[0], small_grads[1], small_grads[2], small_grads[3],...  77.9 us
    dot_general x27, matrix products, product(): return jnp.einsum(form, left, right, preferred_element_type=jnp.float32)  54.9 us
    psum x1, blocking collectives, shards(): lax.psum((small_grads[0], small_grads[1], small_grads[2], small_grads[3],...  38.7 us
    select_n x14, other arithmetic, lap(): jnp.where(position < mine, new, old)  23.2 us
    all_gather x1, blocking collectives, entering_2(): pieces = jax.tree.map(lambda part: lax.all_gather(part, axis), value)  19.9 us
  transfers between devices with their start and end apart: 4, of which 3 were waited for; matrix products, arithmetic and copies ran while one was open for 5% of the time, Pallas kernels for 0%

commit v1 on v0

v1 whole, which is shorter than its diff:
```python
import functools

import jax
import jax.numpy as jnp
from jax import lax
from jax.experimental import pallas as pl
from jax.experimental.pallas import tpu as pltpu
from jax.sharding import PartitionSpec as P

STRETCH = 256
LAG = 2
MESH = pl.DeviceIdType.MESH


def shifted(value, axis, by):
    count = lax.axis_size(axis)
    pairs = [(i, i + by) for i in range(count) if 0 <= i + by < count]
    return lax.ppermute(value, axis, pairs)


def dot_nn(left, right):
    return jnp.dot(left, right, preferred_element_type=jnp.float32)


def dot_nt(left, right):
    return lax.dot_general(
        left, right, (((1,), (1,)), ((), ())), preferred_element_type=jnp.float32
    )


def dot_tn(left, right):
    return lax.dot_general(
        left, right, (((0,), (0,)), ((), ())), preferred_element_type=jnp.float32
    )


def mixer_kernel(
    count,
    pairs,
    head_dim,
    x_ref,
    g_ref,
    key_ref,
    query_ref,
    key_t_ref,
    query_t_ref,
    cum_row_ref,
    cols_ref,
    total_ref,
    skip_ref,
    mix_ref,
    gkey_ref,
    gquery_ref,
    row_cross_ref,
    step_col_ref,
    cum_col_ref,
    tail_col_ref,
    meet_ref,
    skip_sum_ref,
    gram_ref,
    ggram_ref,
    qextra_ref,
    kextra_ref,
    diag_ref,
    s_ref,
    p_ref,
    e_ref,
    b_ref,
    fo_ref,
    bo_ref,
    fsend,
    frecv,
    bsend,
    brecv,
):
    me = lax.axis_index("seq")
    last = count - 1
    wide = 2 * head_dim
    length = key_ref.shape[0]
    barrier = pltpu.get_barrier_semaphore()

    @pl.when(me > 0)
    def _():
        pl.semaphore_signal(barrier, inc=1, device_id={"seq": me - 1}, device_id_type=MESH)

    @pl.when(me < last)
    def _():
        pl.semaphore_signal(barrier, inc=1, device_id={"seq": me + 1}, device_id_type=MESH)

    @pl.when(jnp.logical_and(me > 0, me < last))
    def _():
        pl.semaphore_wait(barrier, 2)

    @pl.when(jnp.logical_or(me == 0, me == last))
    def _():
        pl.semaphore_wait(barrier, 1)

    def fcopy(c):
        return pltpu.make_async_remote_copy(
            src_ref=fo_ref.at[c],
            dst_ref=e_ref.at[c],
            send_sem=fsend.at[c],
            recv_sem=frecv.at[c],
            device_id={"seq": me + 1},
            device_id_type=MESH,
        )

    def bcopy(c):
        return pltpu.make_async_remote_copy(
            src_ref=bo_ref.at[c],
            dst_ref=b_ref.at[c],
            send_sem=bsend.at[c],
            recv_sem=brecv.at[c],
            device_id={"seq": me - 1},
            device_id_type=MESH,
        )

    gram_ref[...] = dot_nt(key_ref[...], query_ref[...])
    ggram_ref[...] = jnp.zeros_like(ggram_ref)
    qextra_ref[...] = jnp.zeros_like(qextra_ref)
    kextra_ref[...] = jnp.zeros_like(kextra_ref)
    step_col_ref[...] = jnp.zeros_like(step_col_ref)
    cum_col_ref[...] = jnp.zeros_like(cum_col_ref)
    tail_col_ref[...] = jnp.zeros_like(tail_col_ref)

    def lanes(c):
        return pl.ds(pl.multiple_of(c * wide, wide), wide)

    def halves(cols, at):
        side = lax.broadcasted_iota(jnp.int32, (length, wide), 1)
        return jnp.where(side < head_dim, cols[:, at : at + 1], cols[:, at + 1 : at + 2])

    def put(ref, head, col):
        side = lax.broadcasted_iota(jnp.int32, ref.shape, 1)
        ref[...] = jnp.where(side == head, col, ref[...])

    def own(c):
        cols = cols_ref[c]
        x = x_ref[:, lanes(c)].astype(jnp.float32)
        g = g_ref[:, lanes(c)].astype(jnp.float32)
        s_ref[c] = dot_nn(key_t_ref[...], (x * halves(cols, 4)).astype(jnp.bfloat16))
        p_ref[c] = dot_nn(query_t_ref[...], (g * halves(cols, 2)).astype(jnp.bfloat16))
        skip_sum_ref[c] = jnp.sum(x * g, axis=0, keepdims=True)

    def inside(c):
        cols = cols_ref[c]
        x = x_ref[:, lanes(c)]
        g = g_ref[:, lanes(c)]
        lower = lax.broadcasted_iota(jnp.int32, (length, length), 0) <= lax.broadcasted_iota(
            jnp.int32, (length, length), 1
        )
        gram = gram_ref[...]
        added = None
        parts = []
        for k in range(2):
            span = slice(k * head_dim, (k + 1) * head_dim)
            xh, gh = x[:, span], g[:, span]
            gap = cum_row_ref[c, k : k + 1, :] - cols[:, k : k + 1]
            decay = jnp.exp(jnp.where(lower, gap, -1e30))
            step = cols[:, 6 + k : 7 + k]
            weights = ((gram * decay) * step).astype(jnp.bfloat16)
            parts.append(dot_nn(weights, gh))
            masked = dot_nt(xh, gh) * decay
            cross = masked * gram
            put(step_col_ref, 2 * c + k, jnp.sum(cross, axis=1, keepdims=True))
            row_cross_ref[c, k : k + 1, :] = jnp.sum(cross * step, axis=0, keepdims=True)
            masked = masked * step
            added = masked if added is None else added + masked
        ggram_ref[...] += added
        diag_ref[:, lanes(c)] = jnp.concatenate(parts, axis=1) + skip_ref[c] * g.astype(jnp.float32)

    def forward(c):
        @pl.when(me > 0)
        def _():
            fcopy(c).wait_recv()

        @pl.when(me == 0)
        def _():
            e_ref[c] = jnp.zeros(e_ref.shape[1:], jnp.float32)

        @pl.when(me < last)
        def _():
            fo_ref[c] = total_ref[c] * e_ref[c] + s_ref[c]
            fcopy(c).start()

    def backward(c):
        @pl.when(me < last)
        def _():
            bcopy(c).wait_recv()

        @pl.when(me == last)
        def _():
            b_ref[c] = jnp.zeros(b_ref.shape[1:], jnp.float32)

        @pl.when(me > 0)
        def _():
            bo_ref[c] = total_ref[c] * b_ref[c] + p_ref[c]
            bcopy(c).start()

    def outside(c):
        cols = cols_ref[c]
        x = x_ref[:, lanes(c)]
        g = g_ref[:, lanes(c)]
        entering = e_ref[c]
        leaving = b_ref[c]
        state_low = entering.astype(jnp.bfloat16)
        grad_low = leaving.astype(jnp.bfloat16)
        meet_ref[c] = jnp.sum(entering * leaving, axis=0, keepdims=True)
        pulled = dot_nn(key_ref[...], grad_low)
        mix_ref[:, lanes(c)] = (diag_ref[:, lanes(c)] + halves(cols, 4) * pulled).astype(jnp.bfloat16)
        key_wide = key_ref[...].astype(jnp.float32)
        query_wide = query_ref[...].astype(jnp.float32)
        qadd, kadd = None, None
        for k in range(2):
            span = slice(k * head_dim, (k + 1) * head_dim)
            read = dot_nt(g[:, span], state_low[:, span]) * cols[:, 2 + k : 3 + k]
            mixed = dot_nt(x[:, span], grad_low[:, span])
            tail = jnp.sum(mixed * key_wide, axis=1, keepdims=True)
            put(tail_col_ref, 2 * c + k, tail)
            put(cum_col_ref, 2 * c + k, jnp.sum(read * query_wide, axis=1, keepdims=True))
            mixed = mixed * cols[:, 4 + k : 5 + k]
            qadd = read if qadd is None else qadd + read
            kadd = mixed if kadd is None else kadd + mixed
        qextra_ref[...] += qadd
        kextra_ref[...] += kadd

    def within(c, work):
        @pl.when(jnp.logical_and(c >= 0, c < pairs))
        def _():
            work(c)

    def tick(t, carry):
        within(t, own)
        within(t - LAG * me, forward)
        within(t - LAG * (last - me), backward)
        within(t, inside)
        within(t - LAG * jnp.maximum(me, last - me), outside)
        return carry

    lax.fori_loop(0, pairs + LAG * last, tick, 0)
    low = ggram_ref[...].astype(jnp.bfloat16)
    gquery_ref[...] = (dot_tn(low, key_ref[...]) + qextra_ref[...]).astype(jnp.bfloat16)
    gkey_ref[...] = (dot_nn(low, query_ref[...]) + kextra_ref[...]).astype(jnp.bfloat16)

    def drain(c, carry):
        @pl.when(me < last)
        def _():
            fcopy(c).wait_send()

        @pl.when(me > 0)
        def _():
            bcopy(c).wait_send()

        return carry

    lax.fori_loop(0, pairs, drain, 0)


def mixer_call(x, g, key, query, cum, step, skip_gain):
    length, width = x.shape
    heads = cum.shape[0]
    head_dim = width // heads
    state = key.shape[1]
    pairs = heads // 2
    wide = 2 * head_dim
    count = lax.axis_size("seq")
    total = cum[:, -1:]
    rise = jnp.exp(cum)
    tail_weight = jnp.exp(total - cum) * step
    cols = jnp.stack([cum, rise, tail_weight, step])
    cols = cols.reshape(4, pairs, 2, length).transpose(1, 3, 0, 2).reshape(pairs, length, 8)
    total_wide = jnp.broadcast_to(jnp.exp(total), (heads, head_dim)).reshape(pairs, 1, wide)
    skip_wide = jnp.broadcast_to(skip_gain[:, None], (heads, head_dim)).reshape(pairs, 1, wide)
    f32 = jnp.float32
    column = jax.ShapeDtypeStruct((length, 128), f32)
    line = jax.ShapeDtypeStruct((pairs, 1, wide), f32)
    small = jax.ShapeDtypeStruct((length, state), jnp.bfloat16)
    vmem = pl.BlockSpec(memory_space=pltpu.VMEM)
    states = pltpu.VMEM((pairs, state, wide), f32)
    sems = pltpu.SemaphoreType.DMA((pairs,))
    return pl.pallas_call(
        functools.partial(mixer_kernel, count, pairs, head_dim),
        out_shape=[
            jax.ShapeDtypeStruct((length, width), jnp.bfloat16),
            small,
            small,
            jax.ShapeDtypeStruct((pairs, 2, length), f32),
            column,
            column,
            column,
            line,
            line,
        ],
        in_specs=[vmem] * 10,
        out_specs=[vmem] * 9,
        scratch_shapes=[
            pltpu.VMEM((length, length), f32),
            pltpu.VMEM((length, length), f32),
            pltpu.VMEM((length, state), f32),
            pltpu.VMEM((length, state), f32),
            pltpu.VMEM((length, width), f32),
        ]
        + [states] * 6
        + [sems] * 4,
        compiler_params=pltpu.CompilerParams(
            collective_id=0, has_side_effects=True, vmem_limit_bytes=56 * 1024 * 1024
        ),
    )(
        x,
        g,
        key,
        query,
        key.T,
        query.T,
        cum.reshape(pairs, 2, length),
        cols,
        total_wide,
        skip_wide,
    )


def sum_kernel(stages, in_ref, out_ref, got_ref, send, recv):
    barrier = pltpu.get_barrier_semaphore()

    def partner(axis, bit):
        me = lax.axis_index(axis)
        return {axis: me + bit - 2 * bit * (lax.div(me, bit) % 2)}

    for axis, bit in stages:
        pl.semaphore_signal(barrier, inc=1, device_id=partner(axis, bit), device_id_type=MESH)
    pl.semaphore_wait(barrier, len(stages))
    out_ref[0] = in_ref[...]
    for at, (axis, bit) in enumerate(stages):
        copy = pltpu.make_async_remote_copy(
            src_ref=out_ref.at[at],
            dst_ref=got_ref.at[at],
            send_sem=send.at[at],
            recv_sem=recv.at[at],
            device_id=partner(axis, bit),
            device_id_type=MESH,
        )
        copy.start()
        copy.wait()
        out_ref[at + 1] = out_ref[at] + got_ref[at]


def summed(value):
    stages = []
    for axis in ("dp", "seq"):
        size, bit = lax.axis_size(axis), 1
        while bit < size:
            stages.append((axis, bit))
            bit *= 2
    n = len(stages)
    vmem = pl.BlockSpec(memory_space=pltpu.VMEM)

    def body(in_ref, final_ref, out_ref, got_ref, send, recv):
        sum_kernel(stages, in_ref, out_ref, got_ref, send, recv)
        final_ref[...] = out_ref[n]

    return pl.pallas_call(
        body,
        out_shape=jax.ShapeDtypeStruct(value.shape, value.dtype),
        in_specs=[vmem],
        out_specs=vmem,
        scratch_shapes=[
            pltpu.VMEM((n + 1, *value.shape), value.dtype),
            pltpu.VMEM((n, *value.shape), value.dtype),
            pltpu.SemaphoreType.DMA((n,)),
            pltpu.SemaphoreType.DMA((n,)),
        ],
        compiler_params=pltpu.CompilerParams(collective_id=1, has_side_effects=True),
    )(value)


def shards(
    mixer_in,
    step_raw,
    key_proj,
    query_proj,
    codec_ids,
    finger_ids,
    fret_ids,
    grad_out,
    decay_log,
    skip_gain,
    codec_bias,
    fret_bias,
    finger_damp,
):
    tokens = mixer_in.shape[1]
    head_count = decay_log.shape[0]
    highest = lax.Precision.HIGHEST
    fingers = finger_ids[0]
    frets = fret_ids[0]
    codec_row = codec_ids[0]
    latest = jnp.stack([fingers[-1], frets[-1]])
    before = shifted(latest, "seq", 1)
    prior_finger = jnp.concatenate([before[0:1], fingers[:-1]])
    prior_fret = jnp.concatenate([before[1:2], frets[:-1]])
    position = lax.axis_index("seq") * tokens + jnp.arange(tokens, dtype=jnp.int32)
    changed = ((fingers != prior_finger) | (frets != prior_fret)).astype(jnp.float32)
    onset_mask = jnp.where(position == 0, 0.0, changed)
    codec_hot = (
        jnp.arange(codec_bias.shape[1], dtype=jnp.int32)[:, None] == codec_row[None, :]
    ).astype(jnp.float32)
    fret_hot = (jnp.arange(fret_bias.shape[1], dtype=jnp.int32)[:, None] == frets[None, :]).astype(
        jnp.float32
    )
    finger_hot = (
        jnp.arange(finger_damp.shape[1], dtype=jnp.int32)[:, None] == fingers[None, :]
    ).astype(jnp.float32)
    pre_step = (
        step_raw[0]
        + jnp.dot(codec_bias, codec_hot, precision=highest)
        + jnp.dot(fret_bias, fret_hot, precision=highest)
    )
    step_size = jax.nn.softplus(pre_step)
    damping = jnp.dot(jax.nn.softplus(finger_damp), finger_hot, precision=highest)
    decay_rate = jnp.exp(decay_log)
    log_decay = -decay_rate[:, None] * step_size - onset_mask[None, :] * damping
    cum = jnp.cumsum(log_decay, axis=1)
    (
        grad_mixer,
        grad_key,
        grad_query,
        row_cross,
        step_col,
        read_col,
        tail_col,
        meet,
        skip_sum,
    ) = mixer_call(mixer_in[0], grad_out[0], key_proj[0], query_proj[0], cum, step_size, skip_gain)
    own_step = step_col[:, :head_count].T
    grad_tail = tail_col[:, :head_count].T
    total = cum[:, -1:]
    tail_decay = jnp.exp(total - cum)
    tail_grad = grad_tail * tail_decay * step_size
    total_grad = jnp.sum(tail_grad, axis=1) + jnp.exp(total[:, 0]) * jnp.sum(
        meet.reshape(head_count, -1), axis=1
    )
    grad_cum = (
        row_cross.reshape(head_count, tokens)
        - step_size * own_step
        + read_col[:, :head_count].T
        - tail_grad
    )
    grad_cum = grad_cum.at[:, -1].add(total_grad)
    grad_step = own_step + grad_tail * tail_decay
    grad_log = jnp.flip(jnp.cumsum(jnp.flip(grad_cum, 1), 1), 1)
    grad_pre = (grad_step - decay_rate[:, None] * grad_log) * jax.nn.sigmoid(pre_step)
    grad_decay = -decay_rate * jnp.sum(step_size * grad_log, axis=1)
    grad_damp = jnp.dot(
        -(onset_mask[None, :] * grad_log), finger_hot.T, precision=highest
    ) * jax.nn.sigmoid(finger_damp)
    grad_codec = jnp.dot(grad_pre, codec_hot.T, precision=highest)
    grad_fret = jnp.dot(grad_pre, fret_hot.T, precision=highest)
    grad_skip = jnp.sum(skip_sum.reshape(head_count, -1), axis=1)
    vocab, frets_n, fingers_n = codec_bias.shape[1], fret_bias.shape[1], finger_damp.shape[1]
    packed = jnp.concatenate(
        [grad_codec, grad_fret, grad_damp, grad_skip[:, None], grad_decay[:, None]], axis=1
    )
    packed = jnp.pad(packed, ((0, 0), (0, -packed.shape[1] % 128)))
    grad_scale = (lax.axis_size("dp") * lax.axis_size("seq") * tokens) ** (-0.5)
    packed = summed(packed) * grad_scale
    a, b, c = vocab, vocab + frets_n, vocab + frets_n + fingers_n
    return (
        grad_mixer[None],
        grad_pre[None],
        grad_key[None],
        grad_query[None],
        packed[:, c + 1],
        packed[:, c],
        packed[:, :a],
        packed[:, a:b],
        packed[:, b:c],
    )


def solution(mesh):
    in_specs = (
        P("dp", "seq", None),
        P("dp", None, "seq"),
        P("dp", "seq", None),
        P("dp", "seq", None),
        P("dp", "seq"),
        P("dp", "seq"),
        P("dp", "seq"),
        P("dp", "seq", None),
        P(),
        P(),
        P(),
        P(),
        P(),
    )
    out_specs = (
        P("dp", "seq", None),
        P("dp", None, "seq"),
        P("dp", "seq", None),
        P("dp", "seq", None),
        P(),
        P(),
        P(),
        P(),
        P(),
    )
    return jax.shard_map(shards, mesh=mesh, in_specs=in_specs, out_specs=out_specs, check_vma=False)
```

time: 608 us -> 159 us (0.26)
  waiting for transfers between devices: 336 us -> 0.01 us
  Pallas kernels: 0 us -> 115 us
  other arithmetic: 75.7 us -> 10 us
  blocking collectives: 58.6 us -> 0 us
  matrix products: 62.1 us -> 4.56 us
  local copies, waits for them, and re-layouts: 51.5 us -> 22.4 us
  between operations: 14.2 us -> 1.02 us
    all_gather x2 -> x0, waiting for transfers between devices: 258 us -> none  [entering_2(): pieces = jax.tree.map(lambda part: lax.all_gather(part, axis), value)]
    pallas_call x0 -> x2, Pallas kernels: none -> 115 us  [the longest x1 85.4 us: mixer_call(): pl.pallas_call(functools.partial(mixer_kernel, count, pairs, head_dim), o...]
    psum x1 -> x0, waiting for transfers between devices: 77.9 us -> none  [shards(): lax.psum((small_grads[0], small_grads[1], small_grads[2], small_grads[3],...]
    dot_general x30 -> x0, matrix products: 57.5 us -> none  [the longest x27 54.9 us: product(): return jnp.einsum(form, left, right, preferred_element_type=jnp.float32)]
    psum x1 -> x0, blocking collectives: 38.7 us -> none  [shards(): lax.psum((small_grads[0], small_grads[1], small_grads[2], small_grads[3],...]
    select_n x14 -> x0, other arithmetic: 23.2 us -> none  [lap(): jnp.where(position < mine, new, old)]
    all_gather x1 -> x0, blocking collectives: 19.9 us -> none  [entering_2(): pieces = jax.tree.map(lambda part: lax.all_gather(part, axis), value)]
    reduce_sum x10 -> x0, local copies, waits for them, and re-layouts: 13.2 us -> none  [the longest x5 6.62 us: one_group(): jnp.sum(tail_grad, axis=1)]
  transfers between devices with their start and end apart: 4 -> 1, of which waited for: 3 -> 0; matrix products, arithmetic and copies ran while one was open for 5% -> 6% of each run, Pallas kernels for 0% -> 0%
where the time goes in v1:
time: 159 us; the launch traced here: 158 us
  Pallas kernels  115 us (72%)
  local copies, waits for them, and re-layouts  22.4 us (14%)
  other arithmetic  10 us (6%)
  starting transfers between devices  4.86 us (3%)
  matrix products  4.56 us (3%)
    pallas_call x1, Pallas kernels, mixer_call(): pl.pallas_call(functools.partial(mixer_kernel, count, pairs, head_dim), o...  85.4 us
    pallas_call x1, Pallas kernels, summed(): pl.pallas_call(body, out_shape=jax.ShapeDtypeStruct(value.shape, value.dt...  29.8 us
    unnamed x30, local copies, waits for them, and re-layouts  9.23 us
    ppermute x1, starting transfers between devices, shifted(): return lax.ppermute(value, axis, pairs)  4.86 us
  transfers between devices with their start and end apart: 1, of which 0 were waited for; matrix products, arithmetic and copies ran while one was open for 6% of the time, Pallas kernels for 0%

profile of v1, /device:TPU:0, one launch (start us, length us, event | category | flops | bytes accessed | tf_op | source)
XLA Modules:
  0.0 158.0 jit_solution(9567198146749000495)
XLA Ops:
  0.7 1.3 slice.83
  1.9 1.2 slice.85
  3.2 1.4 pad_add_fusion
  4.5 4.9 %collective-permute-start = (s32[2]{0:T(128)S(1)}, s32[2]{0:T(128)S(1)}, u32[]{:S(2)}, u32[]{:S(2)}) collective-permute-start(s32[2]{0:T(128)S(1)} %pad_add_fusion), channel_id=1, source_target_pairs={{0,1},{1,2},{2,3},{3,4},{4,5},{5,6},{6,7},{8,9},{9,10},{10,11},{11... | collective-permute-start | bytes 32 | tf_op jit(solution)/shard_map/ppermute | solution.py:18
  9.4 0.9 copy.75
  10.3 0.7 fusion.31
  10.9 1.6 copy.73
  12.5 1.6 copy.74
  14.1 0.7 broadcast_in_dim.52
  14.8 0.1 broadcast_in_dim.53
  14.9 0.7 broadcast_in_dim.54.skip_ref
  15.6 0.8 copy.92
  16.4 1.0 convolution_bitcast_fusion.1
  17.4 1.4 fusion.1
  18.8 0.6 fusion.32
  19.4 2.1 %compare_select_fusion.3 = f32[1,256]{1,0:T(1,128)S(1)} fusion(s32[1,256]{1,0:T(1,128)} %param.21, s32[1,256]{1,0:T(1,128)} %param.20, s32[1,255]{1,0:T(1,128)} %bitcast.98, s32[1,1]{1,0:T(1,128)} %bitcast.15, s32[1,255]{1,0:T(1,128)} %bitcast.96, s32[1,1]{1,0:T(1,128)} %bitcast.16, s32[]{:T(128)S(6)} %mul.72), kind=kLoop, calls=%fused_computation.51 | loop fusion | flops 2304 | bytes 5124 | tf_op jit(solution)/shard_map/jit(_where)/select_n | solution.py:403
  21.5 1.0 fusion.2
  22.6 0.6 reduce-window.14
  23.2 0.2 slice_reduce_fusion.1
  23.4 0.1 broadcast_add_fusion.1
  23.5 0.1 copy.82
  23.7 0.7 reduce_window_sum.47.cum_row_ref
  24.4 0.1 fusion.14
  24.7 0.1 maximum_bitcast_fusion
  24.9 0.1 reshape.168
  25.0 2.2 %copy.88.cols_ref = f32[20,256,8]{2,1,0:T(8,128)} copy(f32[20,256,8]{1,2,0:T(8,128)S(1)} %reshape.168) | data formatting | bytes 327680 | tf_op jit(solution)/shard_map/reshape | solution.py:271
  27.2 0.1 broadcast_in_dim.49
  27.3 0.1 broadcast_in_dim.50
  27.4 0.7 broadcast_in_dim.51.total_ref
  28.1 85.4 %shard_map.196 = (bf16[256,2560]{1,0:T(8,128)(2,1)}, bf16[256,128]{1,0:T(8,128)(2,1)}, bf16[256,128]{1,0:T(8,128)(2,1)}, f32[20,2,256]{2,1,0:T(2,128)}, f32[256,...) custom-call(bf16[256,2560]{1,0:T(8,128)(2,1)} %bitcast.82, ...), custom_call_target="tpu_custom_call" | custom-call | tf_op jit(solution)/shard_map/pallas_call | solution.py:281
  113.5 1.1 multiply_reduce_fusion.1
  114.6 0.8 reshape.169
  115.4 0.1 copy.89
  115.5 0.7 reduce.4
  116.2 0.1 reshape.170
  116.3 0.1 reduce_sum.42
  116.4 1.1 fusion.8
  117.6 0.1 rev.7
  117.7 0.6 reduce-window.16
  118.3 0.2 slice_reduce_fusion
  118.5 0.1 broadcast_add_fusion
  118.6 0.1 copy.91
  118.7 0.1 rev.8
  118.8 0.1 multiply_reduce_fusion
  119.0 0.6 fusion.3
  119.7 0.2 fusion.16
  119.9 0.1 copy.98
  120.0 0.3 convolution_multiply_fusion.1
  120.4 0.1 reshape.173
  120.5 0.1 reduce_sum.44
  120.6 0.1 copy.97
  120.7 0.1 concatenate.22
  120.8 0.7 pad.6.in_ref
  121.5 29.8 %shard_map.197 = f32[40,1152]{1,0:T(8,128)} custom-call(f32[40,1152]{1,0:T(8,128)} %pad.6.in_ref), custom_call_target="tpu_custom_call" | custom-call | tf_op jit(solution)/shard_map/pallas_call | solution.py:361
  151.2 0.9 broadcast_multiply_fusion
  152.2 0.7 slice.111
  152.9 0.1 slice.113
  152.9 0.7 slice_reduce_fusion.2
  153.6 0.7 copy.100
  154.3 0.7 copy.101
  155.0 0.7 copy.99
  155.7 1.1 copy.113
  156.8 0.6 copy.114
  157.4 0.6 copy.115
  (41 shorter events, 0.7 us)
Async XLA Ops:
  0.6 16.8 %copy-start = (f32[40,1024]{1,0:T(8,128)S(1)}, f32[40,1024]{1,0:T(8,128)}, u32[]{:S(2)}) copy-start(f32[40,1024]{1,0:T(8,128)} %param.25) | copy-start | bytes 491524
  4.5 14.3 %collective-permute-start = (s32[2]{0:T(128)S(1)}, s32[2]{0:T(128)S(1)}, u32[]{:S(2)}, u32[]{:S(2)}) collective-permute-start(s32[2]{0:T(128)S(1)} %pad_add_fusion), channel_id=1, source_target_pairs={{0,1},{1,2},{2,3},{3,4},{4,5},{5,6},{6,7},{8,9},{9,10},{10,11},{11... | collective-permute-start | bytes 32 | tf_op jit(solution)/shard_map/ppermute | solution.py:18
  113.5 5.4 %copy-start.2 = (f32[256,128]{1,0:T(8,128)S(1)}, f32[256,128]{1,0:T(8,128)}, u32[]{:S(2)}) copy-start(f32[256,128]{1,0:T(8,128)} %get-tuple-element.31) | copy-start | bytes 393220
  115.5 3.5 %copy-start.8 = (s32[1,256]{1,0:T(1,128)S(1)}, s32[1,256]{1,0:T(1,128)}, u32[]{:S(2)}) copy-start(s32[1,256]{1,0:T(1,128)} %param.19) | copy-start | bytes 3076
  116.4 3.2 %copy-start.5 = (s32[1,256]{1,0:T(1,128)S(1)}, s32[1,256]{1,0:T(1,128)}, u32[]{:S(2)}) copy-start(s32[1,256]{1,0:T(1,128)} %param.21) | copy-start | bytes 3076
  116.4 3.5 %copy-start.9 = (f32[40]{0:T(128)S(1)}, f32[40]{0:T(128)}, u32[]{:S(2)}) copy-start(f32[40]{0:T(128)} %param.23) | copy-start | bytes 484
  116.4 3.6 %copy-start.7 = (s32[1,256]{1,0:T(1,128)S(1)}, s32[1,256]{1,0:T(1,128)}, u32[]{:S(2)}) copy-start(s32[1,256]{1,0:T(1,128)} %param.20) | copy-start | bytes 3076
  117.5 2.8 %copy-start.6 = (f32[20,1,128]{2,1,0:T(1,128)S(1)}, f32[20,1,128]{2,1,0:T(1,128)}, u32[]{:S(2)}) copy-start(f32[20,1,128]{2,1,0:T(1,128)} %get-tuple-element.38) | copy-start | bytes 30724
  119.6 36.0 %copy-start.1 = (bf16[256,2560]{1,0:T(8,128)(2,1)S(1)}, bf16[256,2560]{1,0:T(8,128)(2,1)}, u32[]{:S(2)}) copy-start(bf16[256,2560]{1,0:T(8,128)(2,1)} %get-tuple-element.30) | copy-start | bytes 3932164
  155.7 1.1 copy-start.4
  155.7 1.7 %copy-start.3 = (bf16[256,128]{1,0:T(8,128)(2,1)S(1)}, bf16[256,128]{1,0:T(8,128)(2,1)}, u32[]{:S(2)}) copy-start(bf16[256,128]{1,0:T(8,128)(2,1)} %get-tuple-element.37) | copy-start | bytes 196612

commit v2 on v1

v2 whole, which is shorter than its diff:
```python
import functools

import jax
import jax.numpy as jnp
from jax import lax
from jax.experimental import pallas as pl
from jax.experimental.pallas import tpu as pltpu
from jax.sharding import PartitionSpec as P

LAG = 2
MESH = pl.DeviceIdType.MESH


def dot_nn(left, right):
    return jnp.dot(left, right, preferred_element_type=jnp.float32)


def dot_nt(left, right):
    return lax.dot_general(
        left, right, (((1,), (1,)), ((), ())), preferred_element_type=jnp.float32
    )


def dot_tn(left, right):
    return lax.dot_general(
        left, right, (((0,), (0,)), ((), ())), preferred_element_type=jnp.float32
    )


def pieces(value):
    high = value.astype(jnp.bfloat16)
    rest = value - high.astype(jnp.float32)
    middle = rest.astype(jnp.bfloat16)
    low = (rest - middle.astype(jnp.float32)).astype(jnp.bfloat16)
    return high, middle, low


def exact(form, value, ones):
    high, middle, low = pieces(value)
    return form(low, ones) + form(middle, ones) + form(high, ones)


def soft(value):
    return jnp.maximum(value, 0.0) + jnp.log1p(jnp.exp(-jnp.abs(value)))


def logistic(value):
    return 1.0 / (1.0 + jnp.exp(-value))


FINGER_LANE, DECAY_LANE, SKIP_LANE = 32, 64, 65


def mixer_kernel(
    count,
    pairs,
    head_dim,
    stages,
    scale,
    x_ref,
    g_ref,
    key_ref,
    query_ref,
    raw_ref,
    codec_ref,
    finger_ref,
    fret_ref,
    table_ref,
    small_ref,
    decay_ref,
    skip_ref,
    mix_ref,
    gstep_ref,
    gkey_ref,
    gquery_ref,
    gcodec_ref,
    gsmall_ref,
    gram_ref,
    ggram_ref,
    qextra_ref,
    kextra_ref,
    diag_ref,
    s_ref,
    p_ref,
    e_ref,
    b_ref,
    fo_ref,
    bo_ref,
    rows_ref,
    cols_ref,
    pre_ref,
    row_cross_ref,
    step_col_ref,
    cum_col_ref,
    tail_col_ref,
    meet_ref,
    skip_sum_ref,
    before_ref,
    key_t_ref,
    query_t_ref,
    all_ref,
    half_ref,
    got_half_ref,
    quarter_ref,
    got_ref,
    join_half_ref,
    join_ref,
    fsend,
    frecv,
    bsend,
    brecv,
    isend,
    irecv,
    ssend,
    srecv,
):
    me = lax.axis_index("seq")
    last = count - 1
    wide = 2 * head_dim
    heads = 2 * pairs
    length = key_ref.shape[0]
    barrier = pltpu.get_barrier_semaphore()

    def bit_of(axis, bit):
        return (lax.axis_index(axis) // bit) % 2

    def partner(axis, bit):
        return {axis: lax.axis_index(axis) + bit - 2 * bit * bit_of(axis, bit)}

    others = [stage for stage in stages if stage != ("seq", 1)]

    @pl.when(me > 0)
    def _():
        pl.semaphore_signal(barrier, inc=1, device_id={"seq": me - 1}, device_id_type=MESH)

    @pl.when(me < last)
    def _():
        pl.semaphore_signal(barrier, inc=1, device_id={"seq": me + 1}, device_id_type=MESH)

    for stage in others:
        pl.semaphore_signal(barrier, inc=1, device_id=partner(*stage), device_id_type=MESH)

    @pl.when(jnp.logical_and(me > 0, me < last))
    def _():
        pl.semaphore_wait(barrier, 2 + len(others))

    @pl.when(jnp.logical_or(me == 0, me == last))
    def _():
        pl.semaphore_wait(barrier, 1 + len(others))

    def icopy(at):
        return pltpu.make_async_remote_copy(
            src_ref=(finger_ref, fret_ref)[at],
            dst_ref=before_ref.at[at],
            send_sem=isend.at[at],
            recv_sem=irecv.at[at],
            device_id={"seq": me + 1},
            device_id_type=MESH,
        )

    @pl.when(me < last)
    def _():
        icopy(0).start()
        icopy(1).start()

    codec_hot = (
        lax.broadcasted_iota(jnp.int32, (table_ref.shape[1], length), 0) == codec_ref[...]
    ).astype(jnp.float32).astype(jnp.bfloat16)
    small_row = lax.broadcasted_iota(jnp.int32, (128, length), 0)
    fret_hot = (small_row == fret_ref[...]).astype(jnp.float32).astype(jnp.bfloat16)
    finger_hot = (
        (small_row == finger_ref[...] + FINGER_LANE).astype(jnp.float32).astype(jnp.bfloat16)
    )
    pre_step = (
        raw_ref[0] + exact(dot_nn, table_ref[...], codec_hot) + exact(dot_nn, small_ref[...], fret_hot)
    )
    pre_ref[...] = pre_step
    step = soft(pre_step)
    damping = exact(dot_nn, soft(small_ref[...]), finger_hot)
    head_row = lax.broadcasted_iota(jnp.int32, (heads, 1), 0)
    rate = jnp.zeros((heads, 1), jnp.float32)
    for h in range(heads):
        rate = jnp.where(head_row == h, decay_ref[h], rate)
    rate = jnp.exp(rate)
    key_t_ref[...] = key_ref[...].astype(jnp.float32).T.astype(jnp.bfloat16)
    query_t_ref[...] = query_ref[...].astype(jnp.float32).T.astype(jnp.bfloat16)
    place = lax.broadcasted_iota(jnp.int32, (length, length), 0)
    other = lax.broadcasted_iota(jnp.int32, (length, length), 1)

    @pl.when(me > 0)
    def _():
        pltpu.make_async_remote_copy(
            src_ref=finger_ref,
            dst_ref=before_ref.at[0],
            send_sem=isend.at[0],
            recv_sem=irecv.at[0],
            device_id={"seq": me - 1},
            device_id_type=MESH,
        ).wait_recv()
        pltpu.make_async_remote_copy(
            src_ref=fret_ref,
            dst_ref=before_ref.at[1],
            send_sem=isend.at[1],
            recv_sem=irecv.at[1],
            device_id={"seq": me - 1},
            device_id_type=MESH,
        ).wait_recv()

    @pl.when(me == 0)
    def _():
        before_ref[0] = finger_ref[...]
        before_ref[1] = fret_ref[...]

    spot = lax.broadcasted_iota(jnp.int32, (1, length), 1)

    def changed(ref, at):
        prior = jnp.where(spot == 0, pltpu.roll(before_ref[at], 1, 1), pltpu.roll(ref[...], 1, 1))
        return (ref[...] != prior).astype(jnp.float32)

    onset = jnp.maximum(changed(finger_ref, 0), changed(fret_ref, 1))
    onset = jnp.where(spot + me * length == 0, 0.0, onset)
    log_decay = -rate * step - onset * damping
    until = (place <= other).astype(jnp.float32).astype(jnp.bfloat16)
    cum = exact(dot_nn, log_decay, until)
    rise = jnp.exp(cum)
    tail_decay = jnp.exp(cum[:, length - 1 :] - cum)
    tail_weight = tail_decay * step
    for c in range(pairs):
        both = slice(2 * c, 2 * c + 2)
        rows_ref[c, 0:2, :] = cum[both]
        rows_ref[c, 2:4, :] = rise[both]
        rows_ref[c, 4:6, :] = tail_weight[both]
        rows_ref[c, 6:8, :] = step[both]
    def fcopy(c):
        return pltpu.make_async_remote_copy(
            src_ref=fo_ref.at[c],
            dst_ref=e_ref.at[c],
            send_sem=fsend.at[c],
            recv_sem=frecv.at[c],
            device_id={"seq": me + 1},
            device_id_type=MESH,
        )

    def bcopy(c):
        return pltpu.make_async_remote_copy(
            src_ref=bo_ref.at[c],
            dst_ref=b_ref.at[c],
            send_sem=bsend.at[c],
            recv_sem=brecv.at[c],
            device_id={"seq": me - 1},
            device_id_type=MESH,
        )

    gram_ref[...] = dot_nt(key_ref[...], query_ref[...])
    ggram_ref[...] = jnp.zeros_like(ggram_ref)
    qextra_ref[...] = jnp.zeros_like(qextra_ref)
    kextra_ref[...] = jnp.zeros_like(kextra_ref)
    step_col_ref[...] = jnp.zeros_like(step_col_ref)
    cum_col_ref[...] = jnp.zeros_like(cum_col_ref)
    tail_col_ref[...] = jnp.zeros_like(tail_col_ref)

    def lanes(c):
        return pl.ds(pl.multiple_of(c * wide, wide), wide)

    def halves(cols, at):
        side = lax.broadcasted_iota(jnp.int32, (length, wide), 1)
        return jnp.where(side < head_dim, cols[:, at : at + 1], cols[:, at + 1 : at + 2])

    def put(ref, head, col):
        side = lax.broadcasted_iota(jnp.int32, ref.shape, 1)
        ref[...] = jnp.where(side == head, col, ref[...])

    lane_side = lax.broadcasted_iota(jnp.int32, (1, wide), 1)

    def whole_decay(c):
        end = cols_ref[c, length - 1 : length, :]
        return jnp.where(lane_side < head_dim, end[:, 2:3], end[:, 3:4])

    def split(ref, c, line):
        ref[pl.ds(2 * c, 1), :] = jnp.where(lane_side < head_dim, line, 0.0)
        ref[pl.ds(2 * c + 1, 1), :] = jnp.where(lane_side < head_dim, 0.0, line)

    def own(c):
        cols_ref[c] = rows_ref[c].T
        cols = cols_ref[c]
        x = x_ref[:, lanes(c)].astype(jnp.float32)
        g = g_ref[:, lanes(c)].astype(jnp.float32)
        s_ref[c] = dot_nn(key_t_ref[...], (x * halves(cols, 4)).astype(jnp.bfloat16))
        p_ref[c] = dot_nn(query_t_ref[...], (g * halves(cols, 2)).astype(jnp.bfloat16))
        split(skip_sum_ref, c, jnp.sum(x * g, axis=0, keepdims=True))

    def inside(c):
        cols = cols_ref[c]
        x = x_ref[:, lanes(c)]
        g = g_ref[:, lanes(c)]
        lower = lax.broadcasted_iota(jnp.int32, (length, length), 0) <= lax.broadcasted_iota(
            jnp.int32, (length, length), 1
        )
        gram = gram_ref[...]
        added = None
        parts = []
        for k in range(2):
            span = slice(k * head_dim, (k + 1) * head_dim)
            xh, gh = x[:, span], g[:, span]
            gap = rows_ref[c, k : k + 1, :] - cols[:, k : k + 1]
            decay = jnp.exp(jnp.where(lower, gap, -1e30))
            step = cols[:, 6 + k : 7 + k]
            weights = ((gram * decay) * step).astype(jnp.bfloat16)
            parts.append(dot_nn(weights, gh))
            masked = dot_nt(xh, gh) * decay
            cross = masked * gram
            put(step_col_ref, 2 * c + k, jnp.sum(cross, axis=1, keepdims=True))
            row_cross_ref[pl.ds(2 * c + k, 1), :] = jnp.sum(cross * step, axis=0, keepdims=True)
            masked = masked * step
            added = masked if added is None else added + masked
        ggram_ref[...] += added
        gain = jnp.where(lane_side < head_dim, skip_ref[2 * c], skip_ref[2 * c + 1])
        diag_ref[:, lanes(c)] = jnp.concatenate(parts, axis=1) + gain * g.astype(jnp.float32)

    def forward(c):
        @pl.when(me > 0)
        def _():
            fcopy(c).wait_recv()

        @pl.when(me == 0)
        def _():
            e_ref[c] = jnp.zeros(e_ref.shape[1:], jnp.float32)

        @pl.when(me < last)
        def _():
            fo_ref[c] = whole_decay(c) * e_ref[c] + s_ref[c]
            fcopy(c).start()

    def backward(c):
        @pl.when(me < last)
        def _():
            bcopy(c).wait_recv()

        @pl.when(me == last)
        def _():
            b_ref[c] = jnp.zeros(b_ref.shape[1:], jnp.float32)

        @pl.when(me > 0)
        def _():
            bo_ref[c] = whole_decay(c) * b_ref[c] + p_ref[c]
            bcopy(c).start()

    def outside(c):
        cols = cols_ref[c]
        x = x_ref[:, lanes(c)]
        g = g_ref[:, lanes(c)]
        entering = e_ref[c]
        leaving = b_ref[c]
        state_low = entering.astype(jnp.bfloat16)
        grad_low = leaving.astype(jnp.bfloat16)
        split(meet_ref, c, jnp.sum(entering * leaving, axis=0, keepdims=True))
        pulled = dot_nn(key_ref[...], grad_low)
        mix_ref[:, lanes(c)] = (diag_ref[:, lanes(c)] + halves(cols, 4) * pulled).astype(jnp.bfloat16)
        key_wide = key_ref[...].astype(jnp.float32)
        query_wide = query_ref[...].astype(jnp.float32)
        qadd, kadd = None, None
        for k in range(2):
            span = slice(k * head_dim, (k + 1) * head_dim)
            read = dot_nt(g[:, span], state_low[:, span]) * cols[:, 2 + k : 3 + k]
            mixed = dot_nt(x[:, span], grad_low[:, span])
            tail = jnp.sum(mixed * key_wide, axis=1, keepdims=True)
            put(tail_col_ref, 2 * c + k, tail)
            put(cum_col_ref, 2 * c + k, jnp.sum(read * query_wide, axis=1, keepdims=True))
            mixed = mixed * cols[:, 4 + k : 5 + k]
            qadd = read if qadd is None else qadd + read
            kadd = mixed if kadd is None else kadd + mixed
        qextra_ref[...] += qadd
        kextra_ref[...] += kadd

    def within(c, work):
        @pl.when(jnp.logical_and(c >= 0, c < pairs))
        def _():
            work(c)

    def tick(t, carry):
        within(t, own)
        within(t - LAG * me, forward)
        within(t - LAG * (last - me), backward)
        within(t, inside)
        within(t - LAG * jnp.maximum(me, last - me), outside)
        return carry

    lax.fori_loop(0, pairs + LAG * last, tick, 0)
    low = ggram_ref[...].astype(jnp.bfloat16)
    gquery_ref[...] = (dot_tn(low, key_ref[...]) + qextra_ref[...]).astype(jnp.bfloat16)
    gkey_ref[...] = (dot_nn(low, query_ref[...]) + kextra_ref[...]).astype(jnp.bfloat16)

    @pl.when(me < last)
    def _():
        icopy(0).wait_send()
        icopy(1).wait_send()

    def drain(c, carry):
        @pl.when(me < last)
        def _():
            fcopy(c).wait_send()

        @pl.when(me > 0)
        def _():
            bcopy(c).wait_send()

        return carry

    lax.fori_loop(0, pairs, drain, 0)

    own_step = step_col_ref[...].T[:heads]
    grad_tail = tail_col_ref[...].T[:heads]
    tail_grad = grad_tail * tail_weight
    meet = jnp.sum(meet_ref[...], axis=1, keepdims=True)
    total_grad = jnp.sum(tail_grad, axis=1, keepdims=True) + rise[:, length - 1 :] * meet
    grad_cum = row_cross_ref[...] - step * own_step + cum_col_ref[...].T[:heads] - tail_grad
    grad_cum = jnp.where(spot == length - 1, grad_cum + total_grad, grad_cum)
    after = (place >= other).astype(jnp.float32).astype(jnp.bfloat16)
    grad_log = exact(dot_nn, grad_cum, after)
    grad_pre = (own_step + grad_tail * tail_decay - rate * grad_log) * logistic(pre_ref[...])
    gstep_ref[0] = grad_pre
    grad_codec = exact(dot_nt, grad_pre, codec_hot)
    grad_small = exact(dot_nt, grad_pre, fret_hot) + exact(
        dot_nt, -(onset * grad_log), finger_hot
    ) * logistic(small_ref[...])
    lane = lax.broadcasted_iota(jnp.int32, (1, 128), 1)
    grad_decay = -rate * jnp.sum(step * grad_log, axis=1, keepdims=True)
    grad_skip = jnp.sum(skip_sum_ref[...], axis=1, keepdims=True)
    grad_small = jnp.where(lane == DECAY_LANE, grad_decay, grad_small)
    grad_small = jnp.where(lane == SKIP_LANE, grad_skip, grad_small)
    tall, broad = heads // 8, table_ref.shape[1] // 128 + 1
    for a in range(tall):
        for b in range(broad):
            source = grad_small if b == broad - 1 else grad_codec
            at = 0 if b == broad - 1 else 128 * b
            all_ref[a * broad + b] = source[8 * a : 8 * a + 8, at : at + 128]
    for at in range(tall * broad, all_ref.shape[0]):
        all_ref[at] = jnp.zeros(all_ref.shape[1:], jnp.float32)

    def exchange(at, stage, src, dst):
        copy = pltpu.make_async_remote_copy(
            src_ref=src,
            dst_ref=dst,
            send_sem=ssend.at[at],
            recv_sem=srecv.at[at],
            device_id=partner(*stage),
            device_id_type=MESH,
        )
        copy.start()
        copy.wait()

    half, quarter = half_ref.shape[0], quarter_ref.shape[1]
    first, second = bit_of(*stages[0]), bit_of(*stages[1])
    exchange(0, stages[0], all_ref.at[pl.ds((1 - first) * half, half)], got_half_ref)
    half_ref[...] = all_ref[pl.ds(first * half, half)] + got_half_ref[...]
    exchange(1, stages[1], half_ref.at[pl.ds((1 - second) * quarter, quarter)], got_ref.at[0])
    quarter_ref[0] = half_ref[pl.ds(second * quarter, quarter)] + got_ref[0]
    rest = len(stages) - 2
    for at in range(rest):
        exchange(2 + at, stages[2 + at], quarter_ref.at[at], got_ref.at[at + 1])
        quarter_ref[at + 1] = quarter_ref[at] + got_ref[at + 1]
    mine = pl.ds(second * quarter, quarter)
    join_half_ref[mine] = quarter_ref[rest]
    exchange(2 + rest, stages[1], quarter_ref.at[rest], join_half_ref.at[mine])
    mine = pl.ds(first * half, half)
    join_ref[mine] = join_half_ref[...]
    exchange(3 + rest, stages[0], join_half_ref, join_ref.at[mine])
    for a in range(tall):
        for b in range(broad):
            value = join_ref[a * broad + b] * scale
            if b == broad - 1:
                gsmall_ref[8 * a : 8 * a + 8, :] = value
            else:
                gcodec_ref[8 * a : 8 * a + 8, 128 * b : 128 * b + 128] = value


def shards(
    mixer_in,
    step_raw,
    key_proj,
    query_proj,
    codec_ids,
    finger_ids,
    fret_ids,
    grad_out,
    decay_log,
    skip_gain,
    codec_bias,
    fret_bias,
    finger_damp,
):
    length, width = mixer_in.shape[1:]
    heads = decay_log.shape[0]
    head_dim = width // heads
    state = key_proj.shape[2]
    vocab = codec_bias.shape[1]
    frets, fingers = fret_bias.shape[1], finger_damp.shape[1]
    pairs = heads // 2
    wide = 2 * head_dim
    count = lax.axis_size("seq")
    stages = []
    for axis in ("dp", "seq"):
        bit = 1
        while bit < lax.axis_size(axis):
            stages.append((axis, bit))
            bit *= 2
    scale = float((lax.axis_size("dp") * count * length) ** (-0.5))
    small = jnp.pad(fret_bias, ((0, 0), (0, 128 - frets))) + jnp.pad(
        finger_damp, ((0, 0), (FINGER_LANE, 128 - FINGER_LANE - fingers))
    )
    tiles = (heads // 8) * (vocab // 128 + 1)
    tiles += -tiles % 4
    f32, bf16 = jnp.float32, jnp.bfloat16
    vmem = pl.BlockSpec(memory_space=pltpu.VMEM)
    smem = pl.BlockSpec(memory_space=pltpu.SMEM)
    states = pltpu.VMEM((pairs, state, wide), f32)
    column = pltpu.VMEM((length, 128), f32)
    sems = pltpu.SemaphoreType.DMA((pairs,))
    rounds = len(stages)
    grad_mixer, grad_step, grad_key, grad_query, grad_codec, grad_small = pl.pallas_call(
        functools.partial(mixer_kernel, count, pairs, head_dim, stages, scale),
        out_shape=[
            jax.ShapeDtypeStruct((length, width), bf16),
            jax.ShapeDtypeStruct((1, heads, length), f32),
            jax.ShapeDtypeStruct((length, state), bf16),
            jax.ShapeDtypeStruct((length, state), bf16),
            jax.ShapeDtypeStruct((heads, vocab), f32),
            jax.ShapeDtypeStruct((heads, 128), f32),
        ],
        in_specs=[vmem] * 10 + [smem] * 2,
        out_specs=[vmem] * 6,
        scratch_shapes=[
            pltpu.VMEM((length, length), f32),
            pltpu.VMEM((length, length), f32),
            pltpu.VMEM((length, state), f32),
            pltpu.VMEM((length, state), f32),
            pltpu.VMEM((length, width), f32),
        ]
        + [states] * 6
        + [
            pltpu.VMEM((pairs, 8, length), f32),
            pltpu.VMEM((pairs, length, 8), f32),
            pltpu.VMEM((heads, length), f32),
            pltpu.VMEM((heads, length), f32),
            column,
            column,
            column,
            pltpu.VMEM((heads, wide), f32),
            pltpu.VMEM((heads, wide), f32),
            pltpu.VMEM((2, 1, length), jnp.int32),
            pltpu.VMEM((state, length), bf16),
            pltpu.VMEM((state, length), bf16),
            pltpu.VMEM((tiles, 8, 128), f32),
            pltpu.VMEM((tiles // 2, 8, 128), f32),
            pltpu.VMEM((tiles // 2, 8, 128), f32),
            pltpu.VMEM((rounds - 1, tiles // 4, 8, 128), f32),
            pltpu.VMEM((rounds - 1, tiles // 4, 8, 128), f32),
            pltpu.VMEM((tiles // 2, 8, 128), f32),
            pltpu.VMEM((tiles, 8, 128), f32),
        ]
        + [sems] * 4
        + [pltpu.SemaphoreType.DMA((2,))] * 2
        + [pltpu.SemaphoreType.DMA((rounds + 2,))] * 2,
        compiler_params=pltpu.CompilerParams(
            collective_id=0, has_side_effects=True, vmem_limit_bytes=56 * 1024 * 1024
        ),
    )(
        mixer_in[0],
        grad_out[0],
        key_proj[0],
        query_proj[0],
        step_raw,
        codec_ids,
        finger_ids,
        fret_ids,
        codec_bias,
        small,
        decay_log,
        skip_gain,
    )
    return (
        grad_mixer[None],
        grad_step,
        grad_key[None],
        grad_query[None],
        grad_small[:, DECAY_LANE],
        grad_small[:, SKIP_LANE],
        grad_codec,
        grad_small[:, :frets],
        grad_small[:, FINGER_LANE : FINGER_LANE + fingers],
    )


def solution(mesh):
    in_specs = (
        P("dp", "seq", None),
        P("dp", None, "seq"),
        P("dp", "seq", None),
        P("dp", "seq", None),
        P("dp", "seq"),
        P("dp", "seq"),
        P("dp", "seq"),
        P("dp", "seq", None),
        P(),
        P(),
        P(),
        P(),
        P(),
    )
    out_specs = (
        P("dp", "seq", None),
        P("dp", None, "seq"),
        P("dp", "seq", None),
        P("dp", "seq", None),
        P(),
        P(),
        P(),
        P(),
        P(),
    )
    return jax.shard_map(shards, mesh=mesh, in_specs=in_specs, out_specs=out_specs, check_vma=False)
```

time: 159 us -> 122 us (0.77)
  local copies, waits for them, and re-layouts: 22.4 us -> 11 us
  other arithmetic: 10 us -> 0.69 us
  Pallas kernels: 115 us -> 110 us
  starting transfers between devices: 4.86 us -> 0 us
  matrix products: 4.56 us -> 0 us
    pallas_call x2 -> x1, Pallas kernels: 115 us -> 110 us  [shards(): pl.pallas_call(functools.partial(mixer_kernel, count, pairs, head_dim, st...]
    ppermute x1 -> x0, starting transfers between devices: 4.86 us -> none  [shifted(): return lax.ppermute(value, axis, pairs)]
    dot_general x6 -> x0, matrix products: 4.56 us -> none  [the longest x1 1.37 us: shards(): jnp.dot(codec_bias, codec_hot, precision=highest)]
    reshape x6 -> x0, local copies, waits for them, and re-layouts: 3.41 us -> none  [the longest x2 2.36 us: mixer_call(): cols.reshape(4, pairs, 2, length).transpose(1, 3, 0, 2)]
    another operation x7 -> x0, other arithmetic: 2.8 us -> none
    broadcast_in_dim x8 -> x0, local copies, waits for them, and re-layouts: 2.55 us -> none  [the longest x3 1.51 us: mixer_call(): jnp.broadcast_to(skip_gain[:, None], (heads, head_dim))]
    slice x7 -> x2, local copies, waits for them, and re-layouts: 4.55 us -> 2.31 us  [the longest x1 1.51 us: shards(): grad_small[:, SKIP_LANE]]
    select_n x1 -> x0, other arithmetic: 2.13 us -> none  [shards(): onset_mask = jnp.where(position == 0, 0.0, changed)]
  transfers between devices with their start and end apart: 1 -> 0, of which waited for: 0 -> 0; matrix products, arithmetic and copies ran while one was open for 6% -> 0% of each run, Pallas kernels for 0% -> 0%
where the time goes in v2:
time: 122 us
  Pallas kernels  110 us (90%)
  local copies, waits for them, and re-layouts  11 us (9%)
    pallas_call x1, Pallas kernels, shards(): pl.pallas_call(functools.partial(mixer_kernel, count, pairs, head_dim, st...  110 us
    unnamed x17, local copies, waits for them, and re-layouts  8.71 us

profile of v2, /device:TPU:0, one launch (start us, length us, event | category | flops | bytes accessed | tf_op | source)
XLA Modules:
  0.0 121.9 jit_solution(12063610858831907581)
XLA Ops:
  0.6 0.8 copy.26
  1.4 0.8 copy.27
  2.2 0.7 pad_add_fusion.small_ref
  2.9 109.6 %shard_map.196 = (bf16[256,2560]{1,0:T(8,128)(2,1)}, f32[1,40,256]{2,1,0:T(8,128)}, bf16[256,128]{1,0:T(8,128)(2,1)}, bf16[256,128]{1,0:T(8,128)(2,1)}, f32[40,1024]{1,0:T(8,128)}, /*index=5*/f32[40,128]{1,0:T(8,128)}) custom-call(bf16[256,2560]{1,0:T(8,128)(2,1)} %bitcast.8, bf16[256,2560]{1,0:T(8,128)(2,1)} %bitcast.9, bf16[256,128]{1,0:T(8,128)(2,1)} %bitcast.12, ...), custom_call_target="tpu_custom_call" | custom-call | tf_op jit(solution)/shard_map/pallas_call | solution.py:520
  112.5 1.5 %slice_reduce_fusion = (f32[40]{0:T(128)}, f32[40]{0:T(128)}) fusion(f32[40,128]{1,0:T(8,128)} %get-tuple-element.19), kind=kLoop, calls=%fused_computation | loop fusion | bytes 640 | tf_op jit(solution)/shard_map/slice | solution.py:587
  114.0 1.4 %copy.28 = f32[40,25]{0,1:T(8,128)} copy(f32[40,25]{1,0:T(8,128)} %bitcast.11) | data formatting | bytes 8000
  115.4 0.8 slice.15
  116.2 0.7 copy.29
  116.9 0.0 copy-start.3
  116.9 0.0 copy-start.2
  116.9 0.0 copy-start.1
  116.9 0.0 copy-start
  116.9 2.5 %copy.35 = bf16[1,256,2560]{2,1,0:T(8,128)(2,1)} copy(bf16[1,256,2560]{2,1,0:T(8,128)(2,1)} %bitcast.10) | data formatting | bytes 2621440
  119.4 0.0 copy-done.3
  119.4 0.6 copy.36
  120.0 0.0 copy-done.2
  120.0 0.6 copy.37
  120.6 0.0 copy-done.1
  120.6 0.6 copy.38
  121.3 0.0 copy-done
  121.3 0.7 copy.39
Async XLA Ops:
  116.9 2.5 %copy-start.3 = (f32[1,40,256]{2,1,0:T(8,128)S(1)}, f32[1,40,256]{2,1,0:T(8,128)}, u32[]{:S(2)}) copy-start(f32[1,40,256]{2,1,0:T(8,128)} %get-tuple-element.51) | copy-start | bytes 122884
  116.9 3.1 %copy-start.2 = (bf16[256,128]{1,0:T(8,128)(2,1)S(1)}, bf16[256,128]{1,0:T(8,128)(2,1)}, u32[]{:S(2)}) copy-start(bf16[256,128]{1,0:T(8,128)(2,1)} %get-tuple-element.17) | copy-start | bytes 196612
  116.9 3.8 %copy-start.1 = (bf16[256,128]{1,0:T(8,128)(2,1)S(1)}, bf16[256,128]{1,0:T(8,128)(2,1)}, u32[]{:S(2)}) copy-start(bf16[256,128]{1,0:T(8,128)(2,1)} %get-tuple-element.18) | copy-start | bytes 196612
  116.9 4.4 %copy-start = (f32[40,1024]{1,0:T(8,128)S(1)}, f32[40,1024]{1,0:T(8,128)}, u32[]{:S(2)}) copy-start(f32[40,1024]{1,0:T(8,128)} %get-tuple-element.56) | copy-start | bytes 491524

commit v3 on v2

--- a/solution.py
+++ b/solution.py
@@ -75,6 +75,8 @@
     gquery_ref,
     gcodec_ref,
     gsmall_ref,
+    gfret_ref,
+    gfinger_ref,
     gram_ref,
     ggram_ref,
     qextra_ref,
@@ -293,27 +295,37 @@
         cols = cols_ref[c]
         x = x_ref[:, lanes(c)]
         g = g_ref[:, lanes(c)]
-        lower = lax.broadcasted_iota(jnp.int32, (length, length), 0) <= lax.broadcasted_iota(
-            jnp.int32, (length, length), 1
-        )
-        gram = gram_ref[...]
-        added = None
+        mid = length // 2
         parts = []
+        added = [None, None]
         for k in range(2):
             span = slice(k * head_dim, (k + 1) * head_dim)
             xh, gh = x[:, span], g[:, span]
-            gap = rows_ref[c, k : k + 1, :] - cols[:, k : k + 1]
-            decay = jnp.exp(jnp.where(lower, gap, -1e30))
-            step = cols[:, 6 + k : 7 + k]
-            weights = ((gram * decay) * step).astype(jnp.bfloat16)
-            parts.append(dot_nn(weights, gh))
-            masked = dot_nt(xh, gh) * decay
-            cross = masked * gram
-            put(step_col_ref, 2 * c + k, jnp.sum(cross, axis=1, keepdims=True))
-            row_cross_ref[pl.ds(2 * c + k, 1), :] = jnp.sum(cross * step, axis=0, keepdims=True)
-            masked = masked * step
-            added = masked if added is None else added + masked
-        ggram_ref[...] += added
+            mixes, sums, rows = [], [], []
+            for part in range(2):
+                own_rows, start = slice(part * mid, (part + 1) * mid), part * mid
+                gram = gram_ref[own_rows, start:]
+                lower = lax.broadcasted_iota(jnp.int32, gram.shape, 0) <= lax.broadcasted_iota(
+                    jnp.int32, gram.shape, 1
+                )
+                gap = rows_ref[c, k : k + 1, start:] - cols[own_rows, k : k + 1]
+                decay = jnp.exp(jnp.where(lower, gap, -1e30))
+                step = cols[own_rows, 6 + k : 7 + k]
+                weights = ((gram * decay) * step).astype(jnp.bfloat16)
+                mixes.append(dot_nn(weights, gh[start:]))
+                masked = dot_nt(xh[own_rows], gh[start:]) * decay
+                cross = masked * gram
+                sums.append(jnp.sum(cross, axis=1, keepdims=True))
+                rows.append(jnp.sum(cross * step, axis=0, keepdims=True))
+                masked = masked * step
+                added[part] = masked if added[part] is None else added[part] + masked
+            parts.append(jnp.concatenate(mixes, axis=0))
+            put(step_col_ref, 2 * c + k, jnp.concatenate(sums, axis=0))
+            row_cross_ref[pl.ds(2 * c + k, 1), :] = jnp.concatenate(
+                [rows[0][:, :mid], rows[0][:, mid:] + rows[1]], axis=1
+            )
+        ggram_ref[:mid, :] += added[0]
+        ggram_ref[mid:, mid:] += added[1]
         gain = jnp.where(lane_side < head_dim, skip_ref[2 * c], skip_ref[2 * c + 1])
         diag_ref[:, lanes(c)] = jnp.concatenate(parts, axis=1) + gain * g.astype(jnp.float32)
 
@@ -469,7 +481,10 @@
         for b in range(broad):
             value = join_ref[a * broad + b] * scale
             if b == broad - 1:
-                gsmall_ref[8 * a : 8 * a + 8, :] = value
+                rows = slice(8 * a, 8 * a + 8)
+                gsmall_ref[rows, :] = value
+                gfret_ref[rows, :] = value[:, : gfret_ref.shape[1]]
+                gfinger_ref[rows, :] = value[:, FINGER_LANE : FINGER_LANE + gfinger_ref.shape[1]]
             else:
                 gcodec_ref[8 * a : 8 * a + 8, 128 * b : 128 * b + 128] = value
 
@@ -517,7 +532,7 @@
     column = pltpu.VMEM((length, 128), f32)
     sems = pltpu.SemaphoreType.DMA((pairs,))
     rounds = len(stages)
-    grad_mixer, grad_step, grad_key, grad_query, grad_codec, grad_small = pl.pallas_call(
+    grad_mixer, grad_step, grad_key, grad_query, grad_codec, grad_small, grad_fret, grad_finger = pl.pallas_call(
         functools.partial(mixer_kernel, count, pairs, head_dim, stages, scale),
         out_shape=[
             jax.ShapeDtypeStruct((length, width), bf16),
@@ -526,9 +541,11 @@
             jax.ShapeDtypeStruct((length, state), bf16),
             jax.ShapeDtypeStruct((heads, vocab), f32),
             jax.ShapeDtypeStruct((heads, 128), f32),
+            jax.ShapeDtypeStruct((heads, frets), f32),
+            jax.ShapeDtypeStruct((heads, fingers), f32),
         ],
         in_specs=[vmem] * 10 + [smem] * 2,
-        out_specs=[vmem] * 6,
+        out_specs=[vmem] * 8,
         scratch_shapes=[
             pltpu.VMEM((length, length), f32),
             pltpu.VMEM((length, length), f32),
@@ -586,8 +603,8 @@
         grad_small[:, DECAY_LANE],
         grad_small[:, SKIP_LANE],
         grad_codec,
-        grad_small[:, :frets],
-        grad_small[:, FINGER_LANE : FINGER_LANE + fingers],
+        grad_fret,
+        grad_finger,
     )
 
 

time: 122 us -> 122 us (level)
  no operation moved by 1% of the time
where the time goes in v3:
time: 122 us
  Pallas kernels  110 us (90%)
  local copies, waits for them, and re-layouts  10.9 us (9%)
    pallas_call x1, Pallas kernels, shards(): pl.pallas_call(functools.partial(mixer_kernel, count, pairs, head_dim, st...  110 us
    unnamed x17, local copies, waits for them, and re-layouts  9.43 us

profile of v3, /device:TPU:0, one launch (start us, length us, event | category | flops | bytes accessed | tf_op | source)
XLA Modules:
  0.0 121.9 jit_solution(11319557101264374487)
XLA Ops:
  0.6 0.8 copy.26
  1.4 0.8 copy.27
  2.2 0.7 pad_add_fusion.small_ref
  2.9 109.6 %shard_map.196 = (bf16[256,2560]{1,0:T(8,128)(2,1)}, f32[1,40,256]{2,1,0:T(8,128)}, bf16[256,128]{1,0:T(8,128)(2,1)}, bf16[256,128]{1,0:T(8,128)(2,1)}, f32[40,1...) custom-call(bf16[256,2560]{1,0:T(8,128)(2,1)} %bitcast.7, bf16[256,2560]{1,0:T(8,128)(2,1)} %bitcast.8, ...), custom_call_target="tpu_custom_call" | custom-call | tf_op jit(solution)/shard_map/pallas_call | solution.py:535
  112.5 1.5 %slice_reduce_fusion = (f32[40]{0:T(128)}, f32[40]{0:T(128)}) fusion(f32[40,128]{1,0:T(8,128)} %get-tuple-element.21), kind=kLoop, calls=%fused_computation | loop fusion | bytes 640 | tf_op jit(solution)/shard_map/slice | solution.py:604
  114.0 1.4 %copy.28 = f32[40,25]{0,1:T(8,128)} copy(f32[40,25]{1,0:T(8,128)} %get-tuple-element.41) | data formatting | bytes 8000
  115.4 1.4 %copy.29 = f32[40,5]{0,1:T(8,128)} copy(f32[40,5]{1,0:T(8,128)} %get-tuple-element.42) | data formatting | bytes 1600
  116.8 0.0 copy-start.3
  116.8 0.0 copy-start.2
  116.8 0.0 copy-start.1
  116.8 0.0 copy-start
  116.8 2.5 %copy.35 = bf16[1,256,2560]{2,1,0:T(8,128)(2,1)} copy(bf16[1,256,2560]{2,1,0:T(8,128)(2,1)} %bitcast.9) | data formatting | bytes 2621440
  119.3 0.0 copy-done.3
  119.3 0.6 copy.36
  119.9 0.0 copy-done.2
  119.9 0.6 copy.37
  120.6 0.0 copy-done.1
  120.6 0.6 copy.38
  121.2 0.0 copy-done
  121.2 0.7 copy.39
Async XLA Ops:
  116.8 2.5 %copy-start.3 = (f32[1,40,256]{2,1,0:T(8,128)S(1)}, f32[1,40,256]{2,1,0:T(8,128)}, u32[]{:S(2)}) copy-start(f32[1,40,256]{2,1,0:T(8,128)} %get-tuple-element.55) | copy-start | bytes 122884
  116.8 3.1 %copy-start.2 = (bf16[256,128]{1,0:T(8,128)(2,1)S(1)}, bf16[256,128]{1,0:T(8,128)(2,1)}, u32[]{:S(2)}) copy-start(bf16[256,128]{1,0:T(8,128)(2,1)} %get-tuple-element.19) | copy-start | bytes 196612
  116.8 3.8 %copy-start.1 = (bf16[256,128]{1,0:T(8,128)(2,1)S(1)}, bf16[256,128]{1,0:T(8,128)(2,1)}, u32[]{:S(2)}) copy-start(bf16[256,128]{1,0:T(8,128)(2,1)} %get-tuple-element.20) | copy-start | bytes 196612
  116.8 4.4 %copy-start = (f32[40,1024]{1,0:T(8,128)S(1)}, f32[40,1024]{1,0:T(8,128)}, u32[]{:S(2)}) copy-start(f32[40,1024]{1,0:T(8,128)} %get-tuple-element.60) | copy-start | bytes 491524
